TPU v7x, 256 devices: a whole 4x4x8 slice. The times are simulated.
256 devices in a mesh: section: 16 (over y_hi, z), fsdp: 16 (over x, y_lo, core).
Axes of the slice: x: 4, y: 4 (y_hi: 2, y_lo: 2; y = y_hi * 2 + y_lo), z: 8, core: 2. Of those that a mesh axis runs over, the one named last changes fastest.
Arguments:
- branch_in: bfloat16 [16, 8192, 128], P('section', 'fsdp'), may hold values from -0.0625 to 0.0625
- branch_out: bfloat16 [16, 128, 8192], P('section', None, 'fsdp'), may hold values from -0.5 to 0.5
- down_inputs: bfloat16 [16, 12, 128, 8192], P('section', None, 'fsdp'), may hold values from -6 to 6
- up_inputs: bfloat16 [16, 12, 128, 8192], P('section', None, 'fsdp'), may hold values from -6 to 6
- top_grads: bfloat16 [2, 12, 128, 8192], P(None, None, 'fsdp'), may hold values from -6 to 6
- plan: int32 [2, 12], replicated, may hold values from 0 to 11, each once within a row
- reward_pos: int32 [2, 12, 16], replicated, may hold values from 0 to 7
- reward_cot: float32 [2, 12, 16], replicated, may hold values from -4 to 4
- reward_head: float32 [8192], replicated, may hold values from -5 to 5
Outputs:
- grad_in: float32 [16, 8192, 128], P('section', 'fsdp')
- grad_out: float32 [16, 128, 8192], P('section', None, 'fsdp')
Inputs may be any that keep to these rules, and one draw needn't show every extreme that they name: Each row of plan names every microbatch once.
All inputs are finite; a program needn't handle non-finite values.
Results may differ from a plain program's by a relative error of at most 0.03.
Values may be sent and summed in bfloat16 or wider, within the bound.
No kernel may reach another device: no remote copies, remote signals or barrier semaphores. Data moves between devices by JAX's collectives and lax.ppermute only.
A program may use at most 128 MiB of HBM per device.

v0:
```python
import jax
import jax.numpy as jnp
from jax import lax
from jax.sharding import PartitionSpec as P


def from_partner(value, axis, apart):
    mask = 2**apart
    pairs = [(source, source ^ mask) for source in range(lax.axis_size(axis))]
    return lax.ppermute(value, axis, pairs)


def passed_along(value, axis, steps):
    count = lax.axis_size(axis)
    initial, last = (max(0, -steps), min(count, count - steps))
    return lax.ppermute(value, axis, [(source, source + steps) for source in range(initial, last)])


def branch_grads(inputs, grad, w_in, w_out):
    pre_act = jnp.dot(inputs, w_in, preferred_element_type=jnp.float32)
    sig_val = jax.nn.sigmoid(pre_act)
    hidden = (pre_act * sig_val).astype(jnp.bfloat16)
    grad_hidden = lax.dot_general(
        grad, w_out, (((1,), (1,)), ((), ())), preferred_element_type=jnp.float32
    )
    grad_pre = (grad_hidden * sig_val * (1.0 + pre_act * (1.0 - sig_val))).astype(jnp.bfloat16)
    back_term = lax.dot_general(
        grad_pre, w_in, (((1,), (1,)), ((), ())), preferred_element_type=jnp.float32
    )
    back = (grad.astype(jnp.float32) + back_term).astype(jnp.bfloat16)
    return (hidden, grad_pre, back)


def bit_order(count):
    return list(range(count))


def fetch_mirror(packed):
    hops = lax.axis_size("section").bit_length() - 1
    for bit_index in bit_order(hops):
        packed = from_partner(packed, "section", bit_index)
    return packed


def send_mirror(packed):
    hops = lax.axis_size("section").bit_length() - 1
    for bit_index in bit_order(hops):
        packed = from_partner(packed.astype(jnp.bfloat16), "section", bit_index).astype(
            packed.dtype
        )
    return packed


def slot_pass(
    slot,
    starting,
    received,
    inputs,
    top,
    order,
    positions,
    rewards,
    head,
    row_global,
    seq_len,
    w_in,
    w_out,
    state,
):
    micro_count = inputs.shape[0]
    valid = jnp.logical_and(slot >= 0, slot < micro_count)
    clipped = jnp.clip(slot, 0, micro_count - 1)

    def active(operands):
        acc_in, acc_out = operands
        ident = lax.dynamic_index_in_dim(order, clipped, 0, keepdims=False)
        picked = jnp.arange(micro_count, dtype=jnp.int32) == ident
        pos_now = jnp.sum(jnp.where(picked[:, None], positions, 0), axis=0)
        cot_now = jnp.sum(jnp.where(picked[:, None], rewards, 0.0), axis=0)
        target = jnp.arange(positions.shape[1], dtype=jnp.int32) * seq_len + pos_now
        row_weight = jnp.sum(
            jnp.where(target[:, None] == row_global[None, :], cot_now[:, None], 0.0), axis=0
        )
        top_now = lax.dynamic_index_in_dim(top, clipped, 0, keepdims=False)
        first_grad = (top_now.astype(jnp.float32) + row_weight[:, None] * head[None, :]).astype(
            jnp.bfloat16
        )
        grad = jnp.where(starting, first_grad, received)
        rows_in = lax.dynamic_index_in_dim(inputs, ident, 0, keepdims=False)
        hidden, grad_pre, back = branch_grads(rows_in, grad, w_in, w_out)
        acc_in = acc_in + lax.dot_general(
            rows_in, grad_pre, (((0,), (0,)), ((), ())), preferred_element_type=jnp.float32
        )
        acc_out = acc_out + lax.dot_general(
            hidden, grad, (((0,), (0,)), ((), ())), preferred_element_type=jnp.float32
        )
        return ((acc_in, acc_out), back)

    def resting(operands):
        return (operands, jnp.zeros_like(received))

    return lax.cond(valid, active, resting, state)


def on_device(
    branch_in,
    branch_out,
    down_inputs,
    up_inputs,
    top_grads,
    plan,
    reward_pos,
    reward_cot,
    reward_head,
):
    section_count = lax.axis_size("section")
    section_idx = lax.axis_index("section")
    fsdp_count = lax.axis_size("fsdp")
    micro_count = down_inputs.shape[1]
    local_rows = down_inputs.shape[2]
    width = down_inputs.shape[3]
    seq_count = reward_pos.shape[2]
    seq_len = local_rows * fsdp_count // seq_count
    row_global = lax.axis_index("fsdp") * local_rows + jnp.arange(local_rows, dtype=jnp.int32)
    own_in_shard = branch_in[0]
    own_out_shard = branch_out[0]
    packed_own = jnp.stack([own_in_shard.reshape(own_out_shard.shape), own_out_shard])
    packed_far = fetch_mirror(packed_own)
    far_in_shard = packed_far[0].reshape(own_in_shard.shape)
    far_out_shard = packed_far[1]
    own_in, own_out = (
        lax.all_gather(own_in_shard, "fsdp", axis=0, tiled=True),
        lax.all_gather(own_out_shard, "fsdp", axis=1, tiled=True),
    )
    far_in, far_out = (
        lax.all_gather(far_in_shard, "fsdp", axis=0, tiled=True),
        lax.all_gather(far_out_shard, "fsdp", axis=1, tiled=True),
    )
    zero_in = jnp.zeros(own_in.shape, jnp.float32)
    zero_out = jnp.zeros(own_out.shape, jnp.float32)
    zero_rows = jnp.zeros((local_rows, width), jnp.bfloat16)
    down_state = (zero_in, zero_out)
    up_state = (zero_in, zero_out)

    def advance(step_idx, carry):
        recv_down, recv_up, state_down, state_up = carry
        slot_down = step_idx - (section_count - 1 - section_idx)
        slot_up = step_idx - section_idx
        state_down, back_down = slot_pass(
            slot_down,
            section_idx == section_count - 1,
            recv_down,
            down_inputs[0],
            top_grads[0],
            plan[0],
            reward_pos[0],
            reward_cot[0],
            reward_head,
            row_global,
            seq_len,
            own_in,
            own_out,
            state_down,
        )
        state_up, back_up = slot_pass(
            slot_up,
            section_idx == 0,
            recv_up,
            up_inputs[0],
            top_grads[1],
            plan[1],
            reward_pos[1],
            reward_cot[1],
            reward_head,
            row_global,
            seq_len,
            far_in,
            far_out,
            state_up,
        )
        recv_down = passed_along(back_down, "section", -1)
        recv_up = passed_along(back_up, "section", 1)
        return (recv_down, recv_up, state_down, state_up)

    carry = lax.fori_loop(
        0, section_count + micro_count - 1, advance, (zero_rows, zero_rows, down_state, up_state)
    )
    state_down = carry[2]
    state_up = carry[3]
    shares = (
        lax.psum_scatter(
            state_down[0].astype(jnp.bfloat16), "fsdp", scatter_dimension=0, tiled=True
        ).astype(jnp.float32),
        lax.psum_scatter(
            state_down[1].astype(jnp.bfloat16), "fsdp", scatter_dimension=1, tiled=True
        ).astype(jnp.float32),
        lax.psum_scatter(
            state_up[0].astype(jnp.bfloat16), "fsdp", scatter_dimension=0, tiled=True
        ).astype(jnp.float32),
        lax.psum_scatter(
            state_up[1].astype(jnp.bfloat16), "fsdp", scatter_dimension=1, tiled=True
        ).astype(jnp.float32),
    )
    packed_up = jnp.stack([shares[2].reshape(shares[3].shape), shares[3]])
    packed_back = send_mirror(packed_up)
    grad_in = shares[0] + packed_back[0].reshape(shares[0].shape)
    grad_out = shares[1] + packed_back[1]
    return (grad_in[None], grad_out[None])


def solution(mesh):
    in_specs = (
        P("section", "fsdp", None),
        P("section", None, "fsdp"),
        P("section", None, "fsdp", None),
        P("section", None, "fsdp", None),
        P(None, None, "fsdp", None),
        P(),
        P(),
        P(),
        P(),
    )
    out_specs = (P("section", "fsdp", None), P("section", None, "fsdp"))
    return jax.shard_map(
        on_device, mesh=mesh, in_specs=in_specs, out_specs=out_specs, check_vma=False
    )
```

profile of v0, /device:TPU:16, one launch (start us, length us, event | category | flops | bytes accessed | tf_op | source)
XLA Modules:
  0.0 1438.2 jit_solution(11273259088735241867)
XLA Ops:
  61.6 25.2 %all-gather.10.cloned.1.call-done = bf16[1,128,8192]{2,1,0:T(8,128)(2,1)} async-done(((bf16[1,128,512]{2,1,0:T(8,128)(2,1)}), bf16[1,128,8192]{2,1,0:T(8,128)(2,1)}) %all-gather.10.cloned.1.call-update) | async-done | bytes 2097168 | tf_op jit(solution)/shard_map/all_gather | solution.py:133
  86.9 38.9 %all-gather.8.cloned.1.call-done = bf16[8192,128]{1,0:T(8,128)(2,1)} async-done(((bf16[512,128]{1,0:T(8,128)(2,1)}), bf16[8192,128]{1,0:T(8,128)(2,1)}) %all-gather.8.cloned.1.call-update) | async-done | bytes 2097168 | tf_op jit(solution)/shard_map/all_gather | solution.py:136
  125.7 38.6 %all-gather.14.cloned.1.call-done = bf16[1,128,8192]{2,1,0:T(8,128)(2,1)} async-done(((bf16[1,128,512]{2,1,0:T(8,128)(2,1)}), bf16[1,128,8192]{2,1,0:T(8,128)(2,1)}) %all-gather.14.cloned.1.call-update) | async-done | bytes 2097168 | tf_op jit(solution)/shard_map/all_gather | solution.py:137
  173.9 920.0 %while.25 = (s32[]{:T(128)}, bf16[8,8192]{1,0:T(8,128)(2,1)S(1)}, bf16[8,8192]{1,0:T(8,128)(2,1)S(1)}, f32[8192,128]{1,0:T(8,128)}, f32[128,8192]{1,0:T(8,128)},...) while((s32[]{:T(128)}, bf16[8,8192]{1,0:T(8,128)(2,1)S(1)}, ...), condition=%wide.region_11.12_spmd.clone, body=%wide.region_0.11_spmd.clone.sunk | while | flops 173046048 | bytes 206939488 | solution.py:185
  234.7 19.0 %collective-permute-done.1 = bf16[8,8192]{1,0:T(8,128)(2,1)S(1)} collective-permute-done((bf16[8,8192]{1,0:T(8,128)(2,1)S(1)}, bf16[8,8192]{1,0:T(8,128)(2,1)S(1)}, u32[]{:S(2)}, u32[]{:S(2)}) %collective-permute-start.1) | collective-permute-done | bytes 131104 | tf_op jit(solution)/shard_map/while/body/eval_jaxpr/ppermute | solution.py:16
  253.7 21.6 %collective-permute-start = (bf16[8,8192]{1,0:T(8,128)(2,1)S(1)}, bf16[8,8192]{1,0:T(8,128)(2,1)S(1)}, u32[]{:S(2)}, u32[]{:S(2)}) collective-permute-start(bf16[8,8192]{1,0:T(8,128)(2,1)S(1)} %get-tuple-element.853), channel_id=1, source_target_pairs={{16,0},{32,16},{48,32},{64,48},{80,64},{96,80},{112,96},{128,112},... | collective-permute-start | bytes 393224 | tf_op jit(solution)/shard_map/while/body/eval_jaxpr/ppermute | solution.py:16
  277.7 22.3 %collective-permute-done.1 = bf16[8,8192]{1,0:T(8,128)(2,1)S(1)} collective-permute-done((bf16[8,8192]{1,0:T(8,128)(2,1)S(1)}, bf16[8,8192]{1,0:T(8,128)(2,1)S(1)}, u32[]{:S(2)}, u32[]{:S(2)}) %collective-permute-start.1) | collective-permute-done | bytes 131104 | tf_op jit(solution)/shard_map/while/body/eval_jaxpr/ppermute | solution.py:16
  300.1 21.9 %collective-permute-start = (bf16[8,8192]{1,0:T(8,128)(2,1)S(1)}, bf16[8,8192]{1,0:T(8,128)(2,1)S(1)}, u32[]{:S(2)}, u32[]{:S(2)}) collective-permute-start(bf16[8,8192]{1,0:T(8,128)(2,1)S(1)} %get-tuple-element.853), channel_id=1, source_target_pairs={{16,0},{32,16},{48,32},{64,48},{80,64},{96,80},{112,96},{128,112},... | collective-permute-start | bytes 393224 | tf_op jit(solution)/shard_map/while/body/eval_jaxpr/ppermute | solution.py:16
  322.0 19.6 %collective-permute-start.1 = (bf16[8,8192]{1,0:T(8,128)(2,1)S(1)}, bf16[8,8192]{1,0:T(8,128)(2,1)S(1)}, u32[]{:S(2)}, u32[]{:S(2)}) collective-permute-start(bf16[8,8192]{1,0:T(8,128)(2,1)S(1)} %get-tuple-element.854), channel_id=1, source_target_pairs={{0,16},{16,32},{32,48},{48,64},{64,80},{80,96},{96,112},{112,128},... | collective-permute-start | bytes 393224 | tf_op jit(solution)/shard_map/while/body/eval_jaxpr/ppermute | solution.py:16
  348.0 16.6 %conditional.6 = (f32[8192,128]{1,0:T(8,128)}, f32[128,8192]{1,0:T(8,128)}, bf16[8,8192]{1,0:T(8,128)(2,1)S(1)}) conditional(s32[]{:T(128)} %convert_element_type.119, (f32[8192,128]{1,0:T(8,128)}, f32[128,8192]{1,0:T(8,128)}) %tuple.66, (s32[2,12]{1,0:T(2,128)S(1)}, s32[]{:T(128)}, bf16[1,12,8,8192]{3,2,1,0:T(8,128)(2,1)}, pred[]{:T(512)}, ...), branch_computations={%region_1.1_spmd, %region_2.5_spmd} | conditional | flops 86523016 | bytes 102945120 | solution.py:102
  372.4 22.3 %collective-permute-done.1 = bf16[8,8192]{1,0:T(8,128)(2,1)S(1)} collective-permute-done((bf16[8,8192]{1,0:T(8,128)(2,1)S(1)}, bf16[8,8192]{1,0:T(8,128)(2,1)S(1)}, u32[]{:S(2)}, u32[]{:S(2)}) %collective-permute-start.1) | collective-permute-done | bytes 131104 | tf_op jit(solution)/shard_map/while/body/eval_jaxpr/ppermute | solution.py:16
  415.3 18.0 %conditional.7 = (f32[8192,128]{1,0:T(8,128)}, f32[128,8192]{1,0:T(8,128)}, bf16[8,8192]{1,0:T(8,128)(2,1)S(1)}) conditional(s32[]{:T(128)} %convert_element_type.120, (f32[8192,128]{1,0:T(8,128)}, f32[128,8192]{1,0:T(8,128)}) %tuple.68, (s32[2,12]{1,0:T(2,128)S(1)}, s32[]{:T(128)}, bf16[1,12,8,8192]{3,2,1,0:T(8,128)(2,1)}, pred[]{:T(512)}, ...), branch_computations={%region_6.6_spmd, %region_7.10_spmd} | conditional | flops 86523016 | bytes 102945120 | solution.py:102
  462.3 18.0 %conditional.7 = (f32[8192,128]{1,0:T(8,128)}, f32[128,8192]{1,0:T(8,128)}, bf16[8,8192]{1,0:T(8,128)(2,1)S(1)}) conditional(s32[]{:T(128)} %convert_element_type.120, (f32[8192,128]{1,0:T(8,128)}, f32[128,8192]{1,0:T(8,128)}) %tuple.68, (s32[2,12]{1,0:T(2,128)S(1)}, s32[]{:T(128)}, bf16[1,12,8,8192]{3,2,1,0:T(8,128)(2,1)}, pred[]{:T(512)}, ...), branch_computations={%region_6.6_spmd, %region_7.10_spmd} | conditional | flops 86523016 | bytes 102945120 | solution.py:102
  509.2 18.0 %conditional.7 = (f32[8192,128]{1,0:T(8,128)}, f32[128,8192]{1,0:T(8,128)}, bf16[8,8192]{1,0:T(8,128)(2,1)S(1)}) conditional(s32[]{:T(128)} %convert_element_type.120, (f32[8192,128]{1,0:T(8,128)}, f32[128,8192]{1,0:T(8,128)}) %tuple.68, (s32[2,12]{1,0:T(2,128)S(1)}, s32[]{:T(128)}, bf16[1,12,8,8192]{3,2,1,0:T(8,128)(2,1)}, pred[]{:T(512)}, ...), branch_computations={%region_6.6_spmd, %region_7.10_spmd} | conditional | flops 86523016 | bytes 102945120 | solution.py:102
  556.2 18.0 %conditional.7 = (f32[8192,128]{1,0:T(8,128)}, f32[128,8192]{1,0:T(8,128)}, bf16[8,8192]{1,0:T(8,128)(2,1)S(1)}) conditional(s32[]{:T(128)} %convert_element_type.120, (f32[8192,128]{1,0:T(8,128)}, f32[128,8192]{1,0:T(8,128)}) %tuple.68, (s32[2,12]{1,0:T(2,128)S(1)}, s32[]{:T(128)}, bf16[1,12,8,8192]{3,2,1,0:T(8,128)(2,1)}, pred[]{:T(512)}, ...), branch_computations={%region_6.6_spmd, %region_7.10_spmd} | conditional | flops 86523016 | bytes 102945120 | solution.py:102
  603.1 18.0 %conditional.7 = (f32[8192,128]{1,0:T(8,128)}, f32[128,8192]{1,0:T(8,128)}, bf16[8,8192]{1,0:T(8,128)(2,1)S(1)}) conditional(s32[]{:T(128)} %convert_element_type.120, (f32[8192,128]{1,0:T(8,128)}, f32[128,8192]{1,0:T(8,128)}) %tuple.68, (s32[2,12]{1,0:T(2,128)S(1)}, s32[]{:T(128)}, bf16[1,12,8,8192]{3,2,1,0:T(8,128)(2,1)}, pred[]{:T(512)}, ...), branch_computations={%region_6.6_spmd, %region_7.10_spmd} | conditional | flops 86523016 | bytes 102945120 | solution.py:102
  650.1 18.0 %conditional.7 = (f32[8192,128]{1,0:T(8,128)}, f32[128,8192]{1,0:T(8,128)}, bf16[8,8192]{1,0:T(8,128)(2,1)S(1)}) conditional(s32[]{:T(128)} %convert_element_type.120, (f32[8192,128]{1,0:T(8,128)}, f32[128,8192]{1,0:T(8,128)}) %tuple.68, (s32[2,12]{1,0:T(2,128)S(1)}, s32[]{:T(128)}, bf16[1,12,8,8192]{3,2,1,0:T(8,128)(2,1)}, pred[]{:T(512)}, ...), branch_computations={%region_6.6_spmd, %region_7.10_spmd} | conditional | flops 86523016 | bytes 102945120 | solution.py:102
  697.1 18.0 %conditional.7 = (f32[8192,128]{1,0:T(8,128)}, f32[128,8192]{1,0:T(8,128)}, bf16[8,8192]{1,0:T(8,128)(2,1)S(1)}) conditional(s32[]{:T(128)} %convert_element_type.120, (f32[8192,128]{1,0:T(8,128)}, f32[128,8192]{1,0:T(8,128)}) %tuple.68, (s32[2,12]{1,0:T(2,128)S(1)}, s32[]{:T(128)}, bf16[1,12,8,8192]{3,2,1,0:T(8,128)(2,1)}, pred[]{:T(512)}, ...), branch_computations={%region_6.6_spmd, %region_7.10_spmd} | conditional | flops 86523016 | bytes 102945120 | solution.py:102
  744.0 18.0 %conditional.7 = (f32[8192,128]{1,0:T(8,128)}, f32[128,8192]{1,0:T(8,128)}, bf16[8,8192]{1,0:T(8,128)(2,1)S(1)}) conditional(s32[]{:T(128)} %convert_element_type.120, (f32[8192,128]{1,0:T(8,128)}, f32[128,8192]{1,0:T(8,128)}) %tuple.68, (s32[2,12]{1,0:T(2,128)S(1)}, s32[]{:T(128)}, bf16[1,12,8,8192]{3,2,1,0:T(8,128)(2,1)}, pred[]{:T(512)}, ...), branch_computations={%region_6.6_spmd, %region_7.10_spmd} | conditional | flops 86523016 | bytes 102945120 | solution.py:102
  791.0 18.0 %conditional.7 = (f32[8192,128]{1,0:T(8,128)}, f32[128,8192]{1,0:T(8,128)}, bf16[8,8192]{1,0:T(8,128)(2,1)S(1)}) conditional(s32[]{:T(128)} %convert_element_type.120, (f32[8192,128]{1,0:T(8,128)}, f32[128,8192]{1,0:T(8,128)}) %tuple.68, (s32[2,12]{1,0:T(2,128)S(1)}, s32[]{:T(128)}, bf16[1,12,8,8192]{3,2,1,0:T(8,128)(2,1)}, pred[]{:T(512)}, ...), branch_computations={%region_6.6_spmd, %region_7.10_spmd} | conditional | flops 86523016 | bytes 102945120 | solution.py:102
  838.0 18.0 %conditional.7 = (f32[8192,128]{1,0:T(8,128)}, f32[128,8192]{1,0:T(8,128)}, bf16[8,8192]{1,0:T(8,128)(2,1)S(1)}) conditional(s32[]{:T(128)} %convert_element_type.120, (f32[8192,128]{1,0:T(8,128)}, f32[128,8192]{1,0:T(8,128)}) %tuple.68, (s32[2,12]{1,0:T(2,128)S(1)}, s32[]{:T(128)}, bf16[1,12,8,8192]{3,2,1,0:T(8,128)(2,1)}, pred[]{:T(512)}, ...), branch_computations={%region_6.6_spmd, %region_7.10_spmd} | conditional | flops 86523016 | bytes 102945120 | solution.py:102
  884.9 18.0 %conditional.7 = (f32[8192,128]{1,0:T(8,128)}, f32[128,8192]{1,0:T(8,128)}, bf16[8,8192]{1,0:T(8,128)(2,1)S(1)}) conditional(s32[]{:T(128)} %convert_element_type.120, (f32[8192,128]{1,0:T(8,128)}, f32[128,8192]{1,0:T(8,128)}) %tuple.68, (s32[2,12]{1,0:T(2,128)S(1)}, s32[]{:T(128)}, bf16[1,12,8,8192]{3,2,1,0:T(8,128)(2,1)}, pred[]{:T(512)}, ...), branch_computations={%region_6.6_spmd, %region_7.10_spmd} | conditional | flops 86523016 | bytes 102945120 | solution.py:102
  913.4 18.0 %collective-permute-start = (bf16[8,8192]{1,0:T(8,128)(2,1)S(1)}, bf16[8,8192]{1,0:T(8,128)(2,1)S(1)}, u32[]{:S(2)}, u32[]{:S(2)}) collective-permute-start(bf16[8,8192]{1,0:T(8,128)(2,1)S(1)} %get-tuple-element.853), channel_id=1, source_target_pairs={{16,0},{32,16},{48,32},{64,48},{80,64},{96,80},{112,96},{128,112},... | collective-permute-start | bytes 393224 | tf_op jit(solution)/shard_map/while/body/eval_jaxpr/ppermute | solution.py:16
  931.5 18.0 %conditional.7 = (f32[8192,128]{1,0:T(8,128)}, f32[128,8192]{1,0:T(8,128)}, bf16[8,8192]{1,0:T(8,128)(2,1)S(1)}) conditional(s32[]{:T(128)} %convert_element_type.120, (f32[8192,128]{1,0:T(8,128)}, f32[128,8192]{1,0:T(8,128)}) %tuple.68, (s32[2,12]{1,0:T(2,128)S(1)}, s32[]{:T(128)}, bf16[1,12,8,8192]{3,2,1,0:T(8,128)(2,1)}, pred[]{:T(512)}, ...), branch_computations={%region_6.6_spmd, %region_7.10_spmd} | conditional | flops 86523016 | bytes 102945120 | solution.py:102
  961.9 21.9 %collective-permute-start.1 = (bf16[8,8192]{1,0:T(8,128)(2,1)S(1)}, bf16[8,8192]{1,0:T(8,128)(2,1)S(1)}, u32[]{:S(2)}, u32[]{:S(2)}) collective-permute-start(bf16[8,8192]{1,0:T(8,128)(2,1)S(1)} %get-tuple-element.854), channel_id=1, source_target_pairs={{0,16},{16,32},{32,48},{48,64},{64,80},{80,96},{96,112},{112,128},... | collective-permute-start | bytes 393224 | tf_op jit(solution)/shard_map/while/body/eval_jaxpr/ppermute | solution.py:16
  1000.8 18.2 %collective-permute-start.1 = (bf16[8,8192]{1,0:T(8,128)(2,1)S(1)}, bf16[8,8192]{1,0:T(8,128)(2,1)S(1)}, u32[]{:S(2)}, u32[]{:S(2)}) collective-permute-start(bf16[8,8192]{1,0:T(8,128)(2,1)S(1)} %get-tuple-element.854), channel_id=1, source_target_pairs={{0,16},{16,32},{32,48},{48,64},{64,80},{80,96},{96,112},{112,128},... | collective-permute-start | bytes 393224 | tf_op jit(solution)/shard_map/while/body/eval_jaxpr/ppermute | solution.py:16
  1036.1 18.2 %collective-permute-start.1 = (bf16[8,8192]{1,0:T(8,128)(2,1)S(1)}, bf16[8,8192]{1,0:T(8,128)(2,1)S(1)}, u32[]{:S(2)}, u32[]{:S(2)}) collective-permute-start(bf16[8,8192]{1,0:T(8,128)(2,1)S(1)} %get-tuple-element.854), channel_id=1, source_target_pairs={{0,16},{16,32},{32,48},{48,64},{64,80},{80,96},{96,112},{112,128},... | collective-permute-start | bytes 393224 | tf_op jit(solution)/shard_map/while/body/eval_jaxpr/ppermute | solution.py:16
  1071.4 20.0 %collective-permute-start.1 = (bf16[8,8192]{1,0:T(8,128)(2,1)S(1)}, bf16[8,8192]{1,0:T(8,128)(2,1)S(1)}, u32[]{:S(2)}, u32[]{:S(2)}) collective-permute-start(bf16[8,8192]{1,0:T(8,128)(2,1)S(1)} %get-tuple-element.854), channel_id=1, source_target_pairs={{0,16},{16,32},{32,48},{48,64},{64,80},{80,96},{96,112},{112,128},... | collective-permute-start | bytes 393224 | tf_op jit(solution)/shard_map/while/body/eval_jaxpr/ppermute | solution.py:16
  1109.2 115.3 %reduce-scatter.7.cloned.1.call-done = bf16[512,128]{1,0:T(8,128)(2,1)} async-done(((bf16[8192,128]{1,0:T(8,128)(2,1)}), bf16[512,128]{1,0:T(8,128)(2,1)}) %reduce-scatter.7.cloned.1.call-update) | async-done | bytes 131088 | tf_op jit(solution)/shard_map/reduce_scatter | solution.py:197
  1225.5 67.2 %reduce-scatter.9.cloned.1.call-done = bf16[128,512]{1,0:T(8,128)(2,1)} async-done(((bf16[128,8192]{1,0:T(8,128)(2,1)}), bf16[128,512]{1,0:T(8,128)(2,1)}) %reduce-scatter.9.cloned.1.call-update) | async-done | bytes 131088 | tf_op jit(solution)/shard_map/reduce_scatter | solution.py:200
  1340.1 21.4 %reduce-scatter.11.cloned.1.call-done = bf16[128,512]{1,0:T(8,128)(2,1)} async-done(((bf16[128,8192]{1,0:T(8,128)(2,1)}), bf16[128,512]{1,0:T(8,128)(2,1)}) %reduce-scatter.11.cloned.1.call-update) | async-done | bytes 131088 | tf_op jit(solution)/shard_map/reduce_scatter | solution.py:194
  1363.2 66.5 %reduce-scatter.5.cloned.1.call-done = bf16[512,128]{1,0:T(8,128)(2,1)} async-done(((bf16[8192,128]{1,0:T(8,128)(2,1)}), bf16[512,128]{1,0:T(8,128)(2,1)}) %reduce-scatter.5.cloned.1.call-update) | async-done | bytes 131088 | tf_op jit(solution)/shard_map/reduce_scatter | solution.py:191
  (837 shorter events, 957.5 us)
Async XLA Ops:
  7.2 54.4 %all-gather.12.cloned.1.call-start = ((), (), s32[]{:S(2)}) async-start(), calls=%async_computation.10 | async-start | bytes 2228224 | tf_op jit(solution)/shard_map/all_gather | solution.py:132
  7.9 78.9 %all-gather.10.cloned.1.call-start = ((), (), s32[]{:S(2)}) async-start(), calls=%async_computation.9 | async-start | bytes 2228224 | tf_op jit(solution)/shard_map/all_gather | solution.py:133
  8.7 117.0 %all-gather.8.cloned.1.call-start = ((), (), s32[]{:S(2)}) async-start(), calls=%async_computation.4 | async-start | bytes 2228224 | tf_op jit(solution)/shard_map/all_gather | solution.py:136
  60.7 103.6 %all-gather.14.cloned.1.call-start = ((), (), s32[]{:S(2)}) async-start(), calls=%async_computation.11 | async-start | bytes 2228224 | tf_op jit(solution)/shard_map/all_gather | solution.py:137
  61.3 1163.2 %reduce-scatter.7.cloned.1.call-start = ((), (), s32[]{:S(2)}) async-start(), calls=%async_computation.6 | async-start | bytes 2228224 | tf_op jit(solution)/shard_map/reduce_scatter | solution.py:197
  230.5 23.1 %collective-permute-start.1 = (bf16[8,8192]{1,0:T(8,128)(2,1)S(1)}, bf16[8,8192]{1,0:T(8,128)(2,1)S(1)}, u32[]{:S(2)}, u32[]{:S(2)}) collective-permute-start(bf16[8,8192]{1,0:T(8,128)(2,1)S(1)} %get-tuple-element.854), channel_id=1, source_target_pairs={{0,16},{16,32},{32,48},{48,64},{64,80},{80,96},{96,112},{112,128},... | collective-permute-start | bytes 393224 | tf_op jit(solution)/shard_map/while/body/eval_jaxpr/ppermute | solution.py:16
  253.7 24.1 %collective-permute-start = (bf16[8,8192]{1,0:T(8,128)(2,1)S(1)}, bf16[8,8192]{1,0:T(8,128)(2,1)S(1)}, u32[]{:S(2)}, u32[]{:S(2)}) collective-permute-start(bf16[8,8192]{1,0:T(8,128)(2,1)S(1)} %get-tuple-element.853), channel_id=1, source_target_pairs={{16,0},{32,16},{48,32},{64,48},{80,64},{96,80},{112,96},{128,112},... | collective-permute-start | bytes 393224 | tf_op jit(solution)/shard_map/while/body/eval_jaxpr/ppermute | solution.py:16
  275.3 24.8 %collective-permute-start.1 = (bf16[8,8192]{1,0:T(8,128)(2,1)S(1)}, bf16[8,8192]{1,0:T(8,128)(2,1)S(1)}, u32[]{:S(2)}, u32[]{:S(2)}) collective-permute-start(bf16[8,8192]{1,0:T(8,128)(2,1)S(1)} %get-tuple-element.854), channel_id=1, source_target_pairs={{0,16},{16,32},{32,48},{48,64},{64,80},{80,96},{96,112},{112,128},... | collective-permute-start | bytes 393224 | tf_op jit(solution)/shard_map/while/body/eval_jaxpr/ppermute | solution.py:16
  300.1 42.5 %collective-permute-start = (bf16[8,8192]{1,0:T(8,128)(2,1)S(1)}, bf16[8,8192]{1,0:T(8,128)(2,1)S(1)}, u32[]{:S(2)}, u32[]{:S(2)}) collective-permute-start(bf16[8,8192]{1,0:T(8,128)(2,1)S(1)} %get-tuple-element.853), channel_id=1, source_target_pairs={{16,0},{32,16},{48,32},{64,48},{80,64},{96,80},{112,96},{128,112},... | collective-permute-start | bytes 393224 | tf_op jit(solution)/shard_map/while/body/eval_jaxpr/ppermute | solution.py:16
  322.0 26.0 %collective-permute-start.1 = (bf16[8,8192]{1,0:T(8,128)(2,1)S(1)}, bf16[8,8192]{1,0:T(8,128)(2,1)S(1)}, u32[]{:S(2)}, u32[]{:S(2)}) collective-permute-start(bf16[8,8192]{1,0:T(8,128)(2,1)S(1)} %get-tuple-element.854), channel_id=1, source_target_pairs={{0,16},{16,32},{32,48},{48,64},{64,80},{80,96},{96,112},{112,128},... | collective-permute-start | bytes 393224 | tf_op jit(solution)/shard_map/while/body/eval_jaxpr/ppermute | solution.py:16
  370.0 24.8 %collective-permute-start.1 = (bf16[8,8192]{1,0:T(8,128)(2,1)S(1)}, bf16[8,8192]{1,0:T(8,128)(2,1)S(1)}, u32[]{:S(2)}, u32[]{:S(2)}) collective-permute-start(bf16[8,8192]{1,0:T(8,128)(2,1)S(1)} %get-tuple-element.854), channel_id=1, source_target_pairs={{0,16},{16,32},{32,48},{48,64},{64,80},{80,96},{96,112},{112,128},... | collective-permute-start | bytes 393224 | tf_op jit(solution)/shard_map/while/body/eval_jaxpr/ppermute | solution.py:16
  411.4 23.8 %collective-permute-start = (bf16[8,8192]{1,0:T(8,128)(2,1)S(1)}, bf16[8,8192]{1,0:T(8,128)(2,1)S(1)}, u32[]{:S(2)}, u32[]{:S(2)}) collective-permute-start(bf16[8,8192]{1,0:T(8,128)(2,1)S(1)} %get-tuple-element.853), channel_id=1, source_target_pairs={{16,0},{32,16},{48,32},{64,48},{80,64},{96,80},{112,96},{128,112},... | collective-permute-start | bytes 393224 | tf_op jit(solution)/shard_map/while/body/eval_jaxpr/ppermute | solution.py:16
  460.3 23.8 %collective-permute-start = (bf16[8,8192]{1,0:T(8,128)(2,1)S(1)}, bf16[8,8192]{1,0:T(8,128)(2,1)S(1)}, u32[]{:S(2)}, u32[]{:S(2)}) collective-permute-start(bf16[8,8192]{1,0:T(8,128)(2,1)S(1)} %get-tuple-element.853), channel_id=1, source_target_pairs={{16,0},{32,16},{48,32},{64,48},{80,64},{96,80},{112,96},{128,112},... | collective-permute-start | bytes 393224 | tf_op jit(solution)/shard_map/while/body/eval_jaxpr/ppermute | solution.py:16
  507.3 23.8 %collective-permute-start = (bf16[8,8192]{1,0:T(8,128)(2,1)S(1)}, bf16[8,8192]{1,0:T(8,128)(2,1)S(1)}, u32[]{:S(2)}, u32[]{:S(2)}) collective-permute-start(bf16[8,8192]{1,0:T(8,128)(2,1)S(1)} %get-tuple-element.853), channel_id=1, source_target_pairs={{16,0},{32,16},{48,32},{64,48},{80,64},{96,80},{112,96},{128,112},... | collective-permute-start | bytes 393224 | tf_op jit(solution)/shard_map/while/body/eval_jaxpr/ppermute | solution.py:16
  554.3 23.8 %collective-permute-start = (bf16[8,8192]{1,0:T(8,128)(2,1)S(1)}, bf16[8,8192]{1,0:T(8,128)(2,1)S(1)}, u32[]{:S(2)}, u32[]{:S(2)}) collective-permute-start(bf16[8,8192]{1,0:T(8,128)(2,1)S(1)} %get-tuple-element.853), channel_id=1, source_target_pairs={{16,0},{32,16},{48,32},{64,48},{80,64},{96,80},{112,96},{128,112},... | collective-permute-start | bytes 393224 | tf_op jit(solution)/shard_map/while/body/eval_jaxpr/ppermute | solution.py:16
  601.2 23.8 %collective-permute-start = (bf16[8,8192]{1,0:T(8,128)(2,1)S(1)}, bf16[8,8192]{1,0:T(8,128)(2,1)S(1)}, u32[]{:S(2)}, u32[]{:S(2)}) collective-permute-start(bf16[8,8192]{1,0:T(8,128)(2,1)S(1)} %get-tuple-element.853), channel_id=1, source_target_pairs={{16,0},{32,16},{48,32},{64,48},{80,64},{96,80},{112,96},{128,112},... | collective-permute-start | bytes 393224 | tf_op jit(solution)/shard_map/while/body/eval_jaxpr/ppermute | solution.py:16
  648.2 23.8 %collective-permute-start = (bf16[8,8192]{1,0:T(8,128)(2,1)S(1)}, bf16[8,8192]{1,0:T(8,128)(2,1)S(1)}, u32[]{:S(2)}, u32[]{:S(2)}) collective-permute-start(bf16[8,8192]{1,0:T(8,128)(2,1)S(1)} %get-tuple-element.853), channel_id=1, source_target_pairs={{16,0},{32,16},{48,32},{64,48},{80,64},{96,80},{112,96},{128,112},... | collective-permute-start | bytes 393224 | tf_op jit(solution)/shard_map/while/body/eval_jaxpr/ppermute | solution.py:16
  695.2 23.8 %collective-permute-start = (bf16[8,8192]{1,0:T(8,128)(2,1)S(1)}, bf16[8,8192]{1,0:T(8,128)(2,1)S(1)}, u32[]{:S(2)}, u32[]{:S(2)}) collective-permute-start(bf16[8,8192]{1,0:T(8,128)(2,1)S(1)} %get-tuple-element.853), channel_id=1, source_target_pairs={{16,0},{32,16},{48,32},{64,48},{80,64},{96,80},{112,96},{128,112},... | collective-permute-start | bytes 393224 | tf_op jit(solution)/shard_map/while/body/eval_jaxpr/ppermute | solution.py:16
  742.1 23.8 %collective-permute-start = (bf16[8,8192]{1,0:T(8,128)(2,1)S(1)}, bf16[8,8192]{1,0:T(8,128)(2,1)S(1)}, u32[]{:S(2)}, u32[]{:S(2)}) collective-permute-start(bf16[8,8192]{1,0:T(8,128)(2,1)S(1)} %get-tuple-element.853), channel_id=1, source_target_pairs={{16,0},{32,16},{48,32},{64,48},{80,64},{96,80},{112,96},{128,112},... | collective-permute-start | bytes 393224 | tf_op jit(solution)/shard_map/while/body/eval_jaxpr/ppermute | solution.py:16
  789.1 23.8 %collective-permute-start = (bf16[8,8192]{1,0:T(8,128)(2,1)S(1)}, bf16[8,8192]{1,0:T(8,128)(2,1)S(1)}, u32[]{:S(2)}, u32[]{:S(2)}) collective-permute-start(bf16[8,8192]{1,0:T(8,128)(2,1)S(1)} %get-tuple-element.853), channel_id=1, source_target_pairs={{16,0},{32,16},{48,32},{64,48},{80,64},{96,80},{112,96},{128,112},... | collective-permute-start | bytes 393224 | tf_op jit(solution)/shard_map/while/body/eval_jaxpr/ppermute | solution.py:16
  836.0 23.8 %collective-permute-start = (bf16[8,8192]{1,0:T(8,128)(2,1)S(1)}, bf16[8,8192]{1,0:T(8,128)(2,1)S(1)}, u32[]{:S(2)}, u32[]{:S(2)}) collective-permute-start(bf16[8,8192]{1,0:T(8,128)(2,1)S(1)} %get-tuple-element.853), channel_id=1, source_target_pairs={{16,0},{32,16},{48,32},{64,48},{80,64},{96,80},{112,96},{128,112},... | collective-permute-start | bytes 393224 | tf_op jit(solution)/shard_map/while/body/eval_jaxpr/ppermute | solution.py:16
  883.0 23.8 %collective-permute-start = (bf16[8,8192]{1,0:T(8,128)(2,1)S(1)}, bf16[8,8192]{1,0:T(8,128)(2,1)S(1)}, u32[]{:S(2)}, u32[]{:S(2)}) collective-permute-start(bf16[8,8192]{1,0:T(8,128)(2,1)S(1)} %get-tuple-element.853), channel_id=1, source_target_pairs={{16,0},{32,16},{48,32},{64,48},{80,64},{96,80},{112,96},{128,112},... | collective-permute-start | bytes 393224 | tf_op jit(solution)/shard_map/while/body/eval_jaxpr/ppermute | solution.py:16
  913.4 38.0 %collective-permute-start = (bf16[8,8192]{1,0:T(8,128)(2,1)S(1)}, bf16[8,8192]{1,0:T(8,128)(2,1)S(1)}, u32[]{:S(2)}, u32[]{:S(2)}) collective-permute-start(bf16[8,8192]{1,0:T(8,128)(2,1)S(1)} %get-tuple-element.853), channel_id=1, source_target_pairs={{16,0},{32,16},{48,32},{64,48},{80,64},{96,80},{112,96},{128,112},... | collective-permute-start | bytes 393224 | tf_op jit(solution)/shard_map/while/body/eval_jaxpr/ppermute | solution.py:16
  960.0 23.9 %collective-permute-start = (bf16[8,8192]{1,0:T(8,128)(2,1)S(1)}, bf16[8,8192]{1,0:T(8,128)(2,1)S(1)}, u32[]{:S(2)}, u32[]{:S(2)}) collective-permute-start(bf16[8,8192]{1,0:T(8,128)(2,1)S(1)} %get-tuple-element.853), channel_id=1, source_target_pairs={{16,0},{32,16},{48,32},{64,48},{80,64},{96,80},{112,96},{128,112},... | collective-permute-start | bytes 393224 | tf_op jit(solution)/shard_map/while/body/eval_jaxpr/ppermute | solution.py:16
  961.9 24.4 %collective-permute-start.1 = (bf16[8,8192]{1,0:T(8,128)(2,1)S(1)}, bf16[8,8192]{1,0:T(8,128)(2,1)S(1)}, u32[]{:S(2)}, u32[]{:S(2)}) collective-permute-start(bf16[8,8192]{1,0:T(8,128)(2,1)S(1)} %get-tuple-element.854), channel_id=1, source_target_pairs={{0,16},{16,32},{32,48},{48,64},{64,80},{80,96},{96,112},{112,128},... | collective-permute-start | bytes 393224 | tf_op jit(solution)/shard_map/while/body/eval_jaxpr/ppermute | solution.py:16
  998.8 21.2 %collective-permute-start = (bf16[8,8192]{1,0:T(8,128)(2,1)S(1)}, bf16[8,8192]{1,0:T(8,128)(2,1)S(1)}, u32[]{:S(2)}, u32[]{:S(2)}) collective-permute-start(bf16[8,8192]{1,0:T(8,128)(2,1)S(1)} %get-tuple-element.853), channel_id=1, source_target_pairs={{16,0},{32,16},{48,32},{64,48},{80,64},{96,80},{112,96},{128,112},... | collective-permute-start | bytes 393224 | tf_op jit(solution)/shard_map/while/body/eval_jaxpr/ppermute | solution.py:16
  1034.1 21.2 %collective-permute-start = (bf16[8,8192]{1,0:T(8,128)(2,1)S(1)}, bf16[8,8192]{1,0:T(8,128)(2,1)S(1)}, u32[]{:S(2)}, u32[]{:S(2)}) collective-permute-start(bf16[8,8192]{1,0:T(8,128)(2,1)S(1)} %get-tuple-element.853), channel_id=1, source_target_pairs={{16,0},{32,16},{48,32},{64,48},{80,64},{96,80},{112,96},{128,112},... | collective-permute-start | bytes 393224 | tf_op jit(solution)/shard_map/while/body/eval_jaxpr/ppermute | solution.py:16
  1069.4 23.0 %collective-permute-start = (bf16[8,8192]{1,0:T(8,128)(2,1)S(1)}, bf16[8,8192]{1,0:T(8,128)(2,1)S(1)}, u32[]{:S(2)}, u32[]{:S(2)}) collective-permute-start(bf16[8,8192]{1,0:T(8,128)(2,1)S(1)} %get-tuple-element.853), channel_id=1, source_target_pairs={{16,0},{32,16},{48,32},{64,48},{80,64},{96,80},{112,96},{128,112},... | collective-permute-start | bytes 393224 | tf_op jit(solution)/shard_map/while/body/eval_jaxpr/ppermute | solution.py:16
  1071.4 22.5 %collective-permute-start.1 = (bf16[8,8192]{1,0:T(8,128)(2,1)S(1)}, bf16[8,8192]{1,0:T(8,128)(2,1)S(1)}, u32[]{:S(2)}, u32[]{:S(2)}) collective-permute-start(bf16[8,8192]{1,0:T(8,128)(2,1)S(1)} %get-tuple-element.854), channel_id=1, source_target_pairs={{0,16},{16,32},{32,48},{48,64},{64,80},{80,96},{96,112},{112,128},... | collective-permute-start | bytes 393224 | tf_op jit(solution)/shard_map/while/body/eval_jaxpr/ppermute | solution.py:16
  1097.6 195.1 %reduce-scatter.9.cloned.1.call-start = ((), (), s32[]{:S(2)}) async-start(), calls=%async_computation.7 | async-start | bytes 2228224 | tf_op jit(solution)/shard_map/reduce_scatter | solution.py:200
  1101.5 260.0 %reduce-scatter.11.cloned.1.call-start = ((), (), s32[]{:S(2)}) async-start(), calls=%async_computation.8 | async-start | bytes 2228224 | tf_op jit(solution)/shard_map/reduce_scatter | solution.py:194
  1105.4 324.3 %reduce-scatter.5.cloned.1.call-start = ((), (), s32[]{:S(2)}) async-start(), calls=%async_computation.5 | async-start | bytes 2228224 | tf_op jit(solution)/shard_map/reduce_scatter | solution.py:191
  (163 other events, 855.3 us)
Sparse Core Ops, SparseCore 0:
  9.8 38.6 all-gather.11
  50.3 36.4 all-gather.9
  89.3 36.3 all-gather.7
  128.0 36.3 all-gather.13
  1097.8 126.7 reduce-scatter.6
  1226.9 65.8 reduce-scatter.8
  1295.3 66.2 reduce-scatter.10
  1364.1 65.5 reduce-scatter.4
where the time goes:
time: 1440 us
  waiting for transfers between devices  661 us (46%)
  starting transfers between devices  313 us (22%)
  matrix products  199 us (14%)
  local copies, waits for them, and re-layouts  149 us (10%)
  loops' own time  53.4 us (4%)
  other arithmetic  48.8 us (3%)
    ppermute x54, starting transfers between devices, passed_along(): lax.ppermute(value, axis, [(source, source + steps) for source in range(i...  292 us
    ppermute x54, waiting for transfers between devices, passed_along(): lax.ppermute(value, axis, [(source, source + steps) for source in range(i...  211 us
    reduce_scatter x1, waiting for transfers between devices, on_device(): lax.psum_scatter(state_up[0].astype(jnp.bfloat16), 'fsdp', scatter_dimens...  115 us
    cond x240, local copies, waits for them, and re-layouts  81.5 us
    ppermute x8, waiting for transfers between devices, from_partner(): return lax.ppermute(value, axis, pairs)  74.3 us
    dot_general x24, matrix products, active(): lax.dot_general(rows_in, grad_pre, (((0,), (0,)), ((), ())), preferred_el...  73.4 us
    reduce_scatter x1, waiting for transfers between devices, on_device(): lax.psum_scatter(state_up[1].astype(jnp.bfloat16), 'fsdp', scatter_dimens...  67.2 us
    reduce_scatter x1, waiting for transfers between devices, on_device(): lax.psum_scatter(state_down[0].astype(jnp.bfloat16), 'fsdp', scatter_dime...  66.5 us
  transfers between devices with their start and end apart: 70, of which 56 were waited for; matrix products, arithmetic and copies ran while one was open for 12% of the time, Pallas kernels for 0%

commit v1 on v0

--- a/solution.py
+++ b/solution.py
@@ -133,7 +133,9 @@
         lax.all_gather(own_out_shard, "fsdp", axis=1, tiled=True),
     )
     far_in, far_out = (
-        lax.all_gather(far_in_shard, "fsdp", axis=0, tiled=True),
+        jnp.concatenate(
+            lax.all_to_all(jnp.stack([far_in_shard] * lax.axis_size("fsdp")), "fsdp", 0, 0), axis=0
+        ),
         lax.all_gather(far_out_shard, "fsdp", axis=1, tiled=True),
     )
     zero_in = jnp.zeros(own_in.shape, jnp.float32)

time: 1440 us -> 1380 us (0.958)
  waiting for transfers between devices: 661 us -> 600 us
    all_gather x1 -> x0, waiting for transfers between devices: 38.9 us -> none  [on_device(): lax.all_gather(far_in_shard, 'fsdp', axis=0, tiled=True)]
    all_to_all x0 -> x1, waiting for transfers between devices: none -> 31.7 us  [on_device(): lax.all_to_all(jnp.stack([far_in_shard] * lax.axis_size('fsdp')), 'fsdp',...]
    ppermute x54, waiting for transfers between devices: 211 us -> 184 us  [passed_along(): lax.ppermute(value, axis, [(source, source + steps) for source in range(i...]
    all_gather x1, waiting for transfers between devices: 25.2 us -> 2.78 us  [on_device(): lax.all_gather(own_out_shard, 'fsdp', axis=1, tiled=True)]
  transfers between devices with their start and end apart: 70 -> 70, of which waited for: 56 -> 56; matrix products, arithmetic and copies ran while one was open for 12% -> 10% of each run, Pallas kernels for 0% -> 0%
where the time goes in v1:
time: 1380 us; the launch traced here: 1370 us
  waiting for transfers between devices  600 us (43%)
  starting transfers between devices  323 us (23%)
  matrix products  199 us (14%)
  local copies, waits for them, and re-layouts  148 us (11%)
  other arithmetic  45.8 us (3%)
  loops' own time  44.2 us (3%)
  between operations  14.2 us (1%)
    ppermute x54, starting transfers between devices, passed_along(): lax.ppermute(value, axis, [(source, source + steps) for source in range(i...  296 us
    ppermute x54, waiting for transfers between devices, passed_along(): lax.ppermute(value, axis, [(source, source + steps) for source in range(i...  184 us
    reduce_scatter x1, waiting for transfers between devices, on_device(): lax.psum_scatter(state_up[0].astype(jnp.bfloat16), 'fsdp', scatter_dimens...  110 us
    cond x240, local copies, waits for them, and re-layouts  81.6 us
    dot_general x24, matrix products, active(): lax.dot_general(rows_in, grad_pre, (((0,), (0,)), ((), ())), preferred_el...  73.4 us
    ppermute x8, waiting for transfers between devices, from_partner(): return lax.ppermute(value, axis, pairs)  73.2 us
    reduce_scatter x1, waiting for transfers between devices, on_device(): lax.psum_scatter(state_up[1].astype(jnp.bfloat16), 'fsdp', scatter_dimens...  66.8 us
    reduce_scatter x1, waiting for transfers between devices, on_device(): lax.psum_scatter(state_down[0].astype(jnp.bfloat16), 'fsdp', scatter_dime...  66.8 us
  transfers between devices with their start and end apart: 70, of which 56 were waited for; matrix products, arithmetic and copies ran while one was open for 10% of the time, Pallas kernels for 0%

profile of v1, /device:TPU:16, one launch (start us, length us, event | category | flops | bytes accessed | tf_op | source)
XLA Modules:
  0.0 1374.7 jit_solution(14848681605386206604)
XLA Ops:
  67.4 31.7 %all-to-all-done = bf16[16,512,128]{2,1,0:T(8,128)(2,1)S(1)} async-done(((bf16[16,512,128]{2,1,0:T(8,128)(2,1)}), bf16[16,512,128]{2,1,0:T(8,128)(2,1)S(1)}, u32[]{:S(2)}, u32[]{:S(2)}) %all-to-all-start) | async-done | bytes 2097184 | tf_op jit(solution)/shard_map/all_to_all | solution.py:137
  101.8 42.2 %all-gather.11.cloned.1.call-done = bf16[1,128,8192]{2,1,0:T(8,128)(2,1)} async-done(((bf16[1,128,512]{2,1,0:T(8,128)(2,1)}), bf16[1,128,8192]{2,1,0:T(8,128)(2,1)}) %all-gather.11.cloned.1.call-update) | async-done | bytes 2097168 | tf_op jit(solution)/shard_map/all_gather | solution.py:139
  153.4 882.9 %while.25 = (s32[]{:T(128)}, bf16[8,8192]{1,0:T(8,128)(2,1)S(1)}, bf16[8,8192]{1,0:T(8,128)(2,1)S(1)}, f32[8192,128]{1,0:T(8,128)}, f32[128,8192]{1,0:T(8,128)},...) while((s32[]{:T(128)}, bf16[8,8192]{1,0:T(8,128)(2,1)S(1)}, ...), condition=%wide.region_11.12_spmd.clone, body=%wide.region_0.11_spmd.clone.sunk | while | flops 173046048 | bytes 206939488 | solution.py:187
  229.2 19.6 %collective-permute-start = (bf16[8,8192]{1,0:T(8,128)(2,1)S(1)}, bf16[8,8192]{1,0:T(8,128)(2,1)S(1)}, u32[]{:S(2)}, u32[]{:S(2)}) collective-permute-start(bf16[8,8192]{1,0:T(8,128)(2,1)S(1)} %get-tuple-element.853), channel_id=1, source_target_pairs={{16,0},{32,16},{48,32},{64,48},{80,64},{96,80},{112,96},{128,112},... | collective-permute-start | bytes 393224 | tf_op jit(solution)/shard_map/while/body/eval_jaxpr/ppermute | solution.py:16
  251.4 20.4 %collective-permute-done.1 = bf16[8,8192]{1,0:T(8,128)(2,1)S(1)} collective-permute-done((bf16[8,8192]{1,0:T(8,128)(2,1)S(1)}, bf16[8,8192]{1,0:T(8,128)(2,1)S(1)}, u32[]{:S(2)}, u32[]{:S(2)}) %collective-permute-start.1) | collective-permute-done | bytes 131104 | tf_op jit(solution)/shard_map/while/body/eval_jaxpr/ppermute | solution.py:16
  271.9 19.9 %collective-permute-start = (bf16[8,8192]{1,0:T(8,128)(2,1)S(1)}, bf16[8,8192]{1,0:T(8,128)(2,1)S(1)}, u32[]{:S(2)}, u32[]{:S(2)}) collective-permute-start(bf16[8,8192]{1,0:T(8,128)(2,1)S(1)} %get-tuple-element.853), channel_id=1, source_target_pairs={{16,0},{32,16},{48,32},{64,48},{80,64},{96,80},{112,96},{128,112},... | collective-permute-start | bytes 393224 | tf_op jit(solution)/shard_map/while/body/eval_jaxpr/ppermute | solution.py:16
  291.9 34.5 %collective-permute-start.1 = (bf16[8,8192]{1,0:T(8,128)(2,1)S(1)}, bf16[8,8192]{1,0:T(8,128)(2,1)S(1)}, u32[]{:S(2)}, u32[]{:S(2)}) collective-permute-start(bf16[8,8192]{1,0:T(8,128)(2,1)S(1)} %get-tuple-element.854), channel_id=1, source_target_pairs={{0,16},{16,32},{32,48},{48,64},{64,80},{80,96},{96,112},{112,128},... | collective-permute-start | bytes 393224 | tf_op jit(solution)/shard_map/while/body/eval_jaxpr/ppermute | solution.py:16
  328.9 17.3 %conditional.6 = (f32[8192,128]{1,0:T(8,128)}, f32[128,8192]{1,0:T(8,128)}, bf16[8,8192]{1,0:T(8,128)(2,1)S(1)}) conditional(s32[]{:T(128)} %convert_element_type.119, (f32[8192,128]{1,0:T(8,128)}, f32[128,8192]{1,0:T(8,128)}) %tuple.66, (s32[2,12]{1,0:T(2,128)S(1)}, s32[]{:T(128)}, bf16[1,12,8,8192]{3,2,1,0:T(8,128)(2,1)}, pred[]{:T(512)}, ...), branch_computations={%region_1.1_spmd, %region_2.5_spmd} | conditional | flops 86523016 | bytes 102945120 | solution.py:102
  358.8 17.3 %conditional.6 = (f32[8192,128]{1,0:T(8,128)}, f32[128,8192]{1,0:T(8,128)}, bf16[8,8192]{1,0:T(8,128)(2,1)S(1)}) conditional(s32[]{:T(128)} %convert_element_type.119, (f32[8192,128]{1,0:T(8,128)}, f32[128,8192]{1,0:T(8,128)}) %tuple.66, (s32[2,12]{1,0:T(2,128)S(1)}, s32[]{:T(128)}, bf16[1,12,8,8192]{3,2,1,0:T(8,128)(2,1)}, pred[]{:T(512)}, ...), branch_computations={%region_1.1_spmd, %region_2.5_spmd} | conditional | flops 86523016 | bytes 102945120 | solution.py:102
  380.1 16.1 %conditional.7 = (f32[8192,128]{1,0:T(8,128)}, f32[128,8192]{1,0:T(8,128)}, bf16[8,8192]{1,0:T(8,128)(2,1)S(1)}) conditional(s32[]{:T(128)} %convert_element_type.120, (f32[8192,128]{1,0:T(8,128)}, f32[128,8192]{1,0:T(8,128)}) %tuple.68, (s32[2,12]{1,0:T(2,128)S(1)}, s32[]{:T(128)}, bf16[1,12,8,8192]{3,2,1,0:T(8,128)(2,1)}, pred[]{:T(512)}, ...), branch_computations={%region_6.6_spmd, %region_7.10_spmd} | conditional | flops 86523016 | bytes 102945120 | solution.py:102
  406.6 17.3 %conditional.6 = (f32[8192,128]{1,0:T(8,128)}, f32[128,8192]{1,0:T(8,128)}, bf16[8,8192]{1,0:T(8,128)(2,1)S(1)}) conditional(s32[]{:T(128)} %convert_element_type.119, (f32[8192,128]{1,0:T(8,128)}, f32[128,8192]{1,0:T(8,128)}) %tuple.66, (s32[2,12]{1,0:T(2,128)S(1)}, s32[]{:T(128)}, bf16[1,12,8,8192]{3,2,1,0:T(8,128)(2,1)}, pred[]{:T(512)}, ...), branch_computations={%region_1.1_spmd, %region_2.5_spmd} | conditional | flops 86523016 | bytes 102945120 | solution.py:102
  425.9 16.1 %conditional.7 = (f32[8192,128]{1,0:T(8,128)}, f32[128,8192]{1,0:T(8,128)}, bf16[8,8192]{1,0:T(8,128)(2,1)S(1)}) conditional(s32[]{:T(128)} %convert_element_type.120, (f32[8192,128]{1,0:T(8,128)}, f32[128,8192]{1,0:T(8,128)}) %tuple.68, (s32[2,12]{1,0:T(2,128)S(1)}, s32[]{:T(128)}, bf16[1,12,8,8192]{3,2,1,0:T(8,128)(2,1)}, pred[]{:T(512)}, ...), branch_computations={%region_6.6_spmd, %region_7.10_spmd} | conditional | flops 86523016 | bytes 102945120 | solution.py:102
  452.4 17.3 %conditional.6 = (f32[8192,128]{1,0:T(8,128)}, f32[128,8192]{1,0:T(8,128)}, bf16[8,8192]{1,0:T(8,128)(2,1)S(1)}) conditional(s32[]{:T(128)} %convert_element_type.119, (f32[8192,128]{1,0:T(8,128)}, f32[128,8192]{1,0:T(8,128)}) %tuple.66, (s32[2,12]{1,0:T(2,128)S(1)}, s32[]{:T(128)}, bf16[1,12,8,8192]{3,2,1,0:T(8,128)(2,1)}, pred[]{:T(512)}, ...), branch_computations={%region_1.1_spmd, %region_2.5_spmd} | conditional | flops 86523016 | bytes 102945120 | solution.py:102
  471.7 16.1 %conditional.7 = (f32[8192,128]{1,0:T(8,128)}, f32[128,8192]{1,0:T(8,128)}, bf16[8,8192]{1,0:T(8,128)(2,1)S(1)}) conditional(s32[]{:T(128)} %convert_element_type.120, (f32[8192,128]{1,0:T(8,128)}, f32[128,8192]{1,0:T(8,128)}) %tuple.68, (s32[2,12]{1,0:T(2,128)S(1)}, s32[]{:T(128)}, bf16[1,12,8,8192]{3,2,1,0:T(8,128)(2,1)}, pred[]{:T(512)}, ...), branch_computations={%region_6.6_spmd, %region_7.10_spmd} | conditional | flops 86523016 | bytes 102945120 | solution.py:102
  498.2 17.3 %conditional.6 = (f32[8192,128]{1,0:T(8,128)}, f32[128,8192]{1,0:T(8,128)}, bf16[8,8192]{1,0:T(8,128)(2,1)S(1)}) conditional(s32[]{:T(128)} %convert_element_type.119, (f32[8192,128]{1,0:T(8,128)}, f32[128,8192]{1,0:T(8,128)}) %tuple.66, (s32[2,12]{1,0:T(2,128)S(1)}, s32[]{:T(128)}, bf16[1,12,8,8192]{3,2,1,0:T(8,128)(2,1)}, pred[]{:T(512)}, ...), branch_computations={%region_1.1_spmd, %region_2.5_spmd} | conditional | flops 86523016 | bytes 102945120 | solution.py:102
  517.5 16.1 %conditional.7 = (f32[8192,128]{1,0:T(8,128)}, f32[128,8192]{1,0:T(8,128)}, bf16[8,8192]{1,0:T(8,128)(2,1)S(1)}) conditional(s32[]{:T(128)} %convert_element_type.120, (f32[8192,128]{1,0:T(8,128)}, f32[128,8192]{1,0:T(8,128)}) %tuple.68, (s32[2,12]{1,0:T(2,128)S(1)}, s32[]{:T(128)}, bf16[1,12,8,8192]{3,2,1,0:T(8,128)(2,1)}, pred[]{:T(512)}, ...), branch_computations={%region_6.6_spmd, %region_7.10_spmd} | conditional | flops 86523016 | bytes 102945120 | solution.py:102
  544.0 17.3 %conditional.6 = (f32[8192,128]{1,0:T(8,128)}, f32[128,8192]{1,0:T(8,128)}, bf16[8,8192]{1,0:T(8,128)(2,1)S(1)}) conditional(s32[]{:T(128)} %convert_element_type.119, (f32[8192,128]{1,0:T(8,128)}, f32[128,8192]{1,0:T(8,128)}) %tuple.66, (s32[2,12]{1,0:T(2,128)S(1)}, s32[]{:T(128)}, bf16[1,12,8,8192]{3,2,1,0:T(8,128)(2,1)}, pred[]{:T(512)}, ...), branch_computations={%region_1.1_spmd, %region_2.5_spmd} | conditional | flops 86523016 | bytes 102945120 | solution.py:102
  589.8 17.3 %conditional.6 = (f32[8192,128]{1,0:T(8,128)}, f32[128,8192]{1,0:T(8,128)}, bf16[8,8192]{1,0:T(8,128)(2,1)S(1)}) conditional(s32[]{:T(128)} %convert_element_type.119, (f32[8192,128]{1,0:T(8,128)}, f32[128,8192]{1,0:T(8,128)}) %tuple.66, (s32[2,12]{1,0:T(2,128)S(1)}, s32[]{:T(128)}, bf16[1,12,8,8192]{3,2,1,0:T(8,128)(2,1)}, pred[]{:T(512)}, ...), branch_computations={%region_1.1_spmd, %region_2.5_spmd} | conditional | flops 86523016 | bytes 102945120 | solution.py:102
  635.6 17.3 %conditional.6 = (f32[8192,128]{1,0:T(8,128)}, f32[128,8192]{1,0:T(8,128)}, bf16[8,8192]{1,0:T(8,128)(2,1)S(1)}) conditional(s32[]{:T(128)} %convert_element_type.119, (f32[8192,128]{1,0:T(8,128)}, f32[128,8192]{1,0:T(8,128)}) %tuple.66, (s32[2,12]{1,0:T(2,128)S(1)}, s32[]{:T(128)}, bf16[1,12,8,8192]{3,2,1,0:T(8,128)(2,1)}, pred[]{:T(512)}, ...), branch_computations={%region_1.1_spmd, %region_2.5_spmd} | conditional | flops 86523016 | bytes 102945120 | solution.py:102
  681.4 17.3 %conditional.6 = (f32[8192,128]{1,0:T(8,128)}, f32[128,8192]{1,0:T(8,128)}, bf16[8,8192]{1,0:T(8,128)(2,1)S(1)}) conditional(s32[]{:T(128)} %convert_element_type.119, (f32[8192,128]{1,0:T(8,128)}, f32[128,8192]{1,0:T(8,128)}) %tuple.66, (s32[2,12]{1,0:T(2,128)S(1)}, s32[]{:T(128)}, bf16[1,12,8,8192]{3,2,1,0:T(8,128)(2,1)}, pred[]{:T(512)}, ...), branch_computations={%region_1.1_spmd, %region_2.5_spmd} | conditional | flops 86523016 | bytes 102945120 | solution.py:102
  727.2 17.3 %conditional.6 = (f32[8192,128]{1,0:T(8,128)}, f32[128,8192]{1,0:T(8,128)}, bf16[8,8192]{1,0:T(8,128)(2,1)S(1)}) conditional(s32[]{:T(128)} %convert_element_type.119, (f32[8192,128]{1,0:T(8,128)}, f32[128,8192]{1,0:T(8,128)}) %tuple.66, (s32[2,12]{1,0:T(2,128)S(1)}, s32[]{:T(128)}, bf16[1,12,8,8192]{3,2,1,0:T(8,128)(2,1)}, pred[]{:T(512)}, ...), branch_computations={%region_1.1_spmd, %region_2.5_spmd} | conditional | flops 86523016 | bytes 102945120 | solution.py:102
  772.9 17.3 %conditional.6 = (f32[8192,128]{1,0:T(8,128)}, f32[128,8192]{1,0:T(8,128)}, bf16[8,8192]{1,0:T(8,128)(2,1)S(1)}) conditional(s32[]{:T(128)} %convert_element_type.119, (f32[8192,128]{1,0:T(8,128)}, f32[128,8192]{1,0:T(8,128)}) %tuple.66, (s32[2,12]{1,0:T(2,128)S(1)}, s32[]{:T(128)}, bf16[1,12,8,8192]{3,2,1,0:T(8,128)(2,1)}, pred[]{:T(512)}, ...), branch_computations={%region_1.1_spmd, %region_2.5_spmd} | conditional | flops 86523016 | bytes 102945120 | solution.py:102
  818.7 17.3 %conditional.6 = (f32[8192,128]{1,0:T(8,128)}, f32[128,8192]{1,0:T(8,128)}, bf16[8,8192]{1,0:T(8,128)(2,1)S(1)}) conditional(s32[]{:T(128)} %convert_element_type.119, (f32[8192,128]{1,0:T(8,128)}, f32[128,8192]{1,0:T(8,128)}) %tuple.66, (s32[2,12]{1,0:T(2,128)S(1)}, s32[]{:T(128)}, bf16[1,12,8,8192]{3,2,1,0:T(8,128)(2,1)}, pred[]{:T(512)}, ...), branch_computations={%region_1.1_spmd, %region_2.5_spmd} | conditional | flops 86523016 | bytes 102945120 | solution.py:102
  864.6 18.8 %collective-permute-start = (bf16[8,8192]{1,0:T(8,128)(2,1)S(1)}, bf16[8,8192]{1,0:T(8,128)(2,1)S(1)}, u32[]{:S(2)}, u32[]{:S(2)}) collective-permute-start(bf16[8,8192]{1,0:T(8,128)(2,1)S(1)} %get-tuple-element.853), channel_id=1, source_target_pairs={{16,0},{32,16},{48,32},{64,48},{80,64},{96,80},{112,96},{128,112},... | collective-permute-start | bytes 393224 | tf_op jit(solution)/shard_map/while/body/eval_jaxpr/ppermute | solution.py:16
  911.9 19.9 %collective-permute-start.1 = (bf16[8,8192]{1,0:T(8,128)(2,1)S(1)}, bf16[8,8192]{1,0:T(8,128)(2,1)S(1)}, u32[]{:S(2)}, u32[]{:S(2)}) collective-permute-start(bf16[8,8192]{1,0:T(8,128)(2,1)S(1)} %get-tuple-element.854), channel_id=1, source_target_pairs={{0,16},{16,32},{32,48},{48,64},{64,80},{80,96},{96,112},{112,128},... | collective-permute-start | bytes 393224 | tf_op jit(solution)/shard_map/while/body/eval_jaxpr/ppermute | solution.py:16
  948.9 16.3 %collective-permute-start.1 = (bf16[8,8192]{1,0:T(8,128)(2,1)S(1)}, bf16[8,8192]{1,0:T(8,128)(2,1)S(1)}, u32[]{:S(2)}, u32[]{:S(2)}) collective-permute-start(bf16[8,8192]{1,0:T(8,128)(2,1)S(1)} %get-tuple-element.854), channel_id=1, source_target_pairs={{0,16},{16,32},{32,48},{48,64},{64,80},{80,96},{96,112},{112,128},... | collective-permute-start | bytes 393224 | tf_op jit(solution)/shard_map/while/body/eval_jaxpr/ppermute | solution.py:16
  982.2 16.3 %collective-permute-start.1 = (bf16[8,8192]{1,0:T(8,128)(2,1)S(1)}, bf16[8,8192]{1,0:T(8,128)(2,1)S(1)}, u32[]{:S(2)}, u32[]{:S(2)}) collective-permute-start(bf16[8,8192]{1,0:T(8,128)(2,1)S(1)} %get-tuple-element.854), channel_id=1, source_target_pairs={{0,16},{16,32},{32,48},{48,64},{64,80},{80,96},{96,112},{112,128},... | collective-permute-start | bytes 393224 | tf_op jit(solution)/shard_map/while/body/eval_jaxpr/ppermute | solution.py:16
  1016.1 17.7 %collective-permute-start.1 = (bf16[8,8192]{1,0:T(8,128)(2,1)S(1)}, bf16[8,8192]{1,0:T(8,128)(2,1)S(1)}, u32[]{:S(2)}, u32[]{:S(2)}) collective-permute-start(bf16[8,8192]{1,0:T(8,128)(2,1)S(1)} %get-tuple-element.854), channel_id=1, source_target_pairs={{0,16},{16,32},{32,48},{48,64},{64,80},{80,96},{96,112},{112,128},... | collective-permute-start | bytes 393224 | tf_op jit(solution)/shard_map/while/body/eval_jaxpr/ppermute | solution.py:16
  1051.6 109.7 %reduce-scatter.7.cloned.1.call-done = bf16[512,128]{1,0:T(8,128)(2,1)} async-done(((bf16[8192,128]{1,0:T(8,128)(2,1)}), bf16[512,128]{1,0:T(8,128)(2,1)}) %reduce-scatter.7.cloned.1.call-update) | async-done | bytes 131088 | tf_op jit(solution)/shard_map/reduce_scatter | solution.py:199
  1162.3 66.8 %reduce-scatter.9.cloned.1.call-done = bf16[128,512]{1,0:T(8,128)(2,1)} async-done(((bf16[128,8192]{1,0:T(8,128)(2,1)}), bf16[128,512]{1,0:T(8,128)(2,1)}) %reduce-scatter.9.cloned.1.call-update) | async-done | bytes 131088 | tf_op jit(solution)/shard_map/reduce_scatter | solution.py:202
  1276.6 21.2 %reduce-scatter.11.cloned.1.call-done = bf16[128,512]{1,0:T(8,128)(2,1)} async-done(((bf16[128,8192]{1,0:T(8,128)(2,1)}), bf16[128,512]{1,0:T(8,128)(2,1)}) %reduce-scatter.11.cloned.1.call-update) | async-done | bytes 131088 | tf_op jit(solution)/shard_map/reduce_scatter | solution.py:196
  1299.4 66.8 %reduce-scatter.5.cloned.1.call-done = bf16[512,128]{1,0:T(8,128)(2,1)} async-done(((bf16[8192,128]{1,0:T(8,128)(2,1)}), bf16[512,128]{1,0:T(8,128)(2,1)}) %reduce-scatter.5.cloned.1.call-update) | async-done | bytes 131088 | tf_op jit(solution)/shard_map/reduce_scatter | solution.py:193
  (835 shorter events, 923.8 us)
Async XLA Ops:
  7.2 91.9 %all-gather.9.cloned.1.call-start = ((), (), s32[]{:S(2)}) async-start(), calls=%async_computation.10 | async-start | bytes 2228224 | tf_op jit(solution)/shard_map/all_gather | solution.py:132
  7.9 93.9 %all-gather.7.cloned.1.call-start = ((), (), s32[]{:S(2)}) async-start(), calls=%async_computation.9 | async-start | bytes 2228224 | tf_op jit(solution)/shard_map/all_gather | solution.py:133
  8.6 135.4 %all-gather.11.cloned.1.call-start = ((), (), s32[]{:S(2)}) async-start(), calls=%async_computation.11 | async-start | bytes 2228224 | tf_op jit(solution)/shard_map/all_gather | solution.py:139
  61.8 37.2 %all-to-all-start = ((bf16[16,512,128]{2,1,0:T(8,128)(2,1)}), bf16[16,512,128]{2,1,0:T(8,128)(2,1)S(1)}, u32[]{:S(2)}, u32[]{:S(2)}) async-start(bf16[16,512,128]{2,1,0:T(8,128)(2,1)} %stack.15), calls=%async_computation | async-start | bytes 4194304 | tf_op jit(solution)/shard_map/all_to_all | solution.py:137
  67.1 1094.2 %reduce-scatter.7.cloned.1.call-start = ((), (), s32[]{:S(2)}) async-start(), calls=%async_computation.6 | async-start | bytes 2228224 | tf_op jit(solution)/shard_map/reduce_scatter | solution.py:199
  209.2 20.0 %collective-permute-start.1 = (bf16[8,8192]{1,0:T(8,128)(2,1)S(1)}, bf16[8,8192]{1,0:T(8,128)(2,1)S(1)}, u32[]{:S(2)}, u32[]{:S(2)}) collective-permute-start(bf16[8,8192]{1,0:T(8,128)(2,1)S(1)} %get-tuple-element.854), channel_id=1, source_target_pairs={{0,16},{16,32},{32,48},{48,64},{64,80},{80,96},{96,112},{112,128},... | collective-permute-start | bytes 393224 | tf_op jit(solution)/shard_map/while/body/eval_jaxpr/ppermute | solution.py:16
  229.2 22.2 %collective-permute-start = (bf16[8,8192]{1,0:T(8,128)(2,1)S(1)}, bf16[8,8192]{1,0:T(8,128)(2,1)S(1)}, u32[]{:S(2)}, u32[]{:S(2)}) collective-permute-start(bf16[8,8192]{1,0:T(8,128)(2,1)S(1)} %get-tuple-element.853), channel_id=1, source_target_pairs={{16,0},{32,16},{48,32},{64,48},{80,64},{96,80},{112,96},{128,112},... | collective-permute-start | bytes 393224 | tf_op jit(solution)/shard_map/while/body/eval_jaxpr/ppermute | solution.py:16
  249.0 22.9 %collective-permute-start.1 = (bf16[8,8192]{1,0:T(8,128)(2,1)S(1)}, bf16[8,8192]{1,0:T(8,128)(2,1)S(1)}, u32[]{:S(2)}, u32[]{:S(2)}) collective-permute-start(bf16[8,8192]{1,0:T(8,128)(2,1)S(1)} %get-tuple-element.854), channel_id=1, source_target_pairs={{0,16},{16,32},{32,48},{48,64},{64,80},{80,96},{96,112},{112,128},... | collective-permute-start | bytes 393224 | tf_op jit(solution)/shard_map/while/body/eval_jaxpr/ppermute | solution.py:16
  271.9 55.4 %collective-permute-start = (bf16[8,8192]{1,0:T(8,128)(2,1)S(1)}, bf16[8,8192]{1,0:T(8,128)(2,1)S(1)}, u32[]{:S(2)}, u32[]{:S(2)}) collective-permute-start(bf16[8,8192]{1,0:T(8,128)(2,1)S(1)} %get-tuple-element.853), channel_id=1, source_target_pairs={{16,0},{32,16},{48,32},{64,48},{80,64},{96,80},{112,96},{128,112},... | collective-permute-start | bytes 393224 | tf_op jit(solution)/shard_map/while/body/eval_jaxpr/ppermute | solution.py:16
  291.9 37.0 %collective-permute-start.1 = (bf16[8,8192]{1,0:T(8,128)(2,1)S(1)}, bf16[8,8192]{1,0:T(8,128)(2,1)S(1)}, u32[]{:S(2)}, u32[]{:S(2)}) collective-permute-start(bf16[8,8192]{1,0:T(8,128)(2,1)S(1)} %get-tuple-element.854), channel_id=1, source_target_pairs={{0,16},{16,32},{32,48},{48,64},{64,80},{80,96},{96,112},{112,128},... | collective-permute-start | bytes 393224 | tf_op jit(solution)/shard_map/while/body/eval_jaxpr/ppermute | solution.py:16
  376.2 21.9 %collective-permute-start = (bf16[8,8192]{1,0:T(8,128)(2,1)S(1)}, bf16[8,8192]{1,0:T(8,128)(2,1)S(1)}, u32[]{:S(2)}, u32[]{:S(2)}) collective-permute-start(bf16[8,8192]{1,0:T(8,128)(2,1)S(1)} %get-tuple-element.853), channel_id=1, source_target_pairs={{16,0},{32,16},{48,32},{64,48},{80,64},{96,80},{112,96},{128,112},... | collective-permute-start | bytes 393224 | tf_op jit(solution)/shard_map/while/body/eval_jaxpr/ppermute | solution.py:16
  424.0 21.9 %collective-permute-start = (bf16[8,8192]{1,0:T(8,128)(2,1)S(1)}, bf16[8,8192]{1,0:T(8,128)(2,1)S(1)}, u32[]{:S(2)}, u32[]{:S(2)}) collective-permute-start(bf16[8,8192]{1,0:T(8,128)(2,1)S(1)} %get-tuple-element.853), channel_id=1, source_target_pairs={{16,0},{32,16},{48,32},{64,48},{80,64},{96,80},{112,96},{128,112},... | collective-permute-start | bytes 393224 | tf_op jit(solution)/shard_map/while/body/eval_jaxpr/ppermute | solution.py:16
  469.7 21.9 %collective-permute-start = (bf16[8,8192]{1,0:T(8,128)(2,1)S(1)}, bf16[8,8192]{1,0:T(8,128)(2,1)S(1)}, u32[]{:S(2)}, u32[]{:S(2)}) collective-permute-start(bf16[8,8192]{1,0:T(8,128)(2,1)S(1)} %get-tuple-element.853), channel_id=1, source_target_pairs={{16,0},{32,16},{48,32},{64,48},{80,64},{96,80},{112,96},{128,112},... | collective-permute-start | bytes 393224 | tf_op jit(solution)/shard_map/while/body/eval_jaxpr/ppermute | solution.py:16
  515.5 21.9 %collective-permute-start = (bf16[8,8192]{1,0:T(8,128)(2,1)S(1)}, bf16[8,8192]{1,0:T(8,128)(2,1)S(1)}, u32[]{:S(2)}, u32[]{:S(2)}) collective-permute-start(bf16[8,8192]{1,0:T(8,128)(2,1)S(1)} %get-tuple-element.853), channel_id=1, source_target_pairs={{16,0},{32,16},{48,32},{64,48},{80,64},{96,80},{112,96},{128,112},... | collective-permute-start | bytes 393224 | tf_op jit(solution)/shard_map/while/body/eval_jaxpr/ppermute | solution.py:16
  561.3 21.9 %collective-permute-start = (bf16[8,8192]{1,0:T(8,128)(2,1)S(1)}, bf16[8,8192]{1,0:T(8,128)(2,1)S(1)}, u32[]{:S(2)}, u32[]{:S(2)}) collective-permute-start(bf16[8,8192]{1,0:T(8,128)(2,1)S(1)} %get-tuple-element.853), channel_id=1, source_target_pairs={{16,0},{32,16},{48,32},{64,48},{80,64},{96,80},{112,96},{128,112},... | collective-permute-start | bytes 393224 | tf_op jit(solution)/shard_map/while/body/eval_jaxpr/ppermute | solution.py:16
  607.1 21.9 %collective-permute-start = (bf16[8,8192]{1,0:T(8,128)(2,1)S(1)}, bf16[8,8192]{1,0:T(8,128)(2,1)S(1)}, u32[]{:S(2)}, u32[]{:S(2)}) collective-permute-start(bf16[8,8192]{1,0:T(8,128)(2,1)S(1)} %get-tuple-element.853), channel_id=1, source_target_pairs={{16,0},{32,16},{48,32},{64,48},{80,64},{96,80},{112,96},{128,112},... | collective-permute-start | bytes 393224 | tf_op jit(solution)/shard_map/while/body/eval_jaxpr/ppermute | solution.py:16
  652.9 21.9 %collective-permute-start = (bf16[8,8192]{1,0:T(8,128)(2,1)S(1)}, bf16[8,8192]{1,0:T(8,128)(2,1)S(1)}, u32[]{:S(2)}, u32[]{:S(2)}) collective-permute-start(bf16[8,8192]{1,0:T(8,128)(2,1)S(1)} %get-tuple-element.853), channel_id=1, source_target_pairs={{16,0},{32,16},{48,32},{64,48},{80,64},{96,80},{112,96},{128,112},... | collective-permute-start | bytes 393224 | tf_op jit(solution)/shard_map/while/body/eval_jaxpr/ppermute | solution.py:16
  698.7 21.9 %collective-permute-start = (bf16[8,8192]{1,0:T(8,128)(2,1)S(1)}, bf16[8,8192]{1,0:T(8,128)(2,1)S(1)}, u32[]{:S(2)}, u32[]{:S(2)}) collective-permute-start(bf16[8,8192]{1,0:T(8,128)(2,1)S(1)} %get-tuple-element.853), channel_id=1, source_target_pairs={{16,0},{32,16},{48,32},{64,48},{80,64},{96,80},{112,96},{128,112},... | collective-permute-start | bytes 393224 | tf_op jit(solution)/shard_map/while/body/eval_jaxpr/ppermute | solution.py:16
  744.5 21.9 %collective-permute-start = (bf16[8,8192]{1,0:T(8,128)(2,1)S(1)}, bf16[8,8192]{1,0:T(8,128)(2,1)S(1)}, u32[]{:S(2)}, u32[]{:S(2)}) collective-permute-start(bf16[8,8192]{1,0:T(8,128)(2,1)S(1)} %get-tuple-element.853), channel_id=1, source_target_pairs={{16,0},{32,16},{48,32},{64,48},{80,64},{96,80},{112,96},{128,112},... | collective-permute-start | bytes 393224 | tf_op jit(solution)/shard_map/while/body/eval_jaxpr/ppermute | solution.py:16
  790.3 21.9 %collective-permute-start = (bf16[8,8192]{1,0:T(8,128)(2,1)S(1)}, bf16[8,8192]{1,0:T(8,128)(2,1)S(1)}, u32[]{:S(2)}, u32[]{:S(2)}) collective-permute-start(bf16[8,8192]{1,0:T(8,128)(2,1)S(1)} %get-tuple-element.853), channel_id=1, source_target_pairs={{16,0},{32,16},{48,32},{64,48},{80,64},{96,80},{112,96},{128,112},... | collective-permute-start | bytes 393224 | tf_op jit(solution)/shard_map/while/body/eval_jaxpr/ppermute | solution.py:16
  836.1 21.9 %collective-permute-start = (bf16[8,8192]{1,0:T(8,128)(2,1)S(1)}, bf16[8,8192]{1,0:T(8,128)(2,1)S(1)}, u32[]{:S(2)}, u32[]{:S(2)}) collective-permute-start(bf16[8,8192]{1,0:T(8,128)(2,1)S(1)} %get-tuple-element.853), channel_id=1, source_target_pairs={{16,0},{32,16},{48,32},{64,48},{80,64},{96,80},{112,96},{128,112},... | collective-permute-start | bytes 393224 | tf_op jit(solution)/shard_map/while/body/eval_jaxpr/ppermute | solution.py:16
  864.6 36.8 %collective-permute-start = (bf16[8,8192]{1,0:T(8,128)(2,1)S(1)}, bf16[8,8192]{1,0:T(8,128)(2,1)S(1)}, u32[]{:S(2)}, u32[]{:S(2)}) collective-permute-start(bf16[8,8192]{1,0:T(8,128)(2,1)S(1)} %get-tuple-element.853), channel_id=1, source_target_pairs={{16,0},{32,16},{48,32},{64,48},{80,64},{96,80},{112,96},{128,112},... | collective-permute-start | bytes 393224 | tf_op jit(solution)/shard_map/while/body/eval_jaxpr/ppermute | solution.py:16
  909.9 21.9 %collective-permute-start = (bf16[8,8192]{1,0:T(8,128)(2,1)S(1)}, bf16[8,8192]{1,0:T(8,128)(2,1)S(1)}, u32[]{:S(2)}, u32[]{:S(2)}) collective-permute-start(bf16[8,8192]{1,0:T(8,128)(2,1)S(1)} %get-tuple-element.853), channel_id=1, source_target_pairs={{16,0},{32,16},{48,32},{64,48},{80,64},{96,80},{112,96},{128,112},... | collective-permute-start | bytes 393224 | tf_op jit(solution)/shard_map/while/body/eval_jaxpr/ppermute | solution.py:16
  911.9 22.4 %collective-permute-start.1 = (bf16[8,8192]{1,0:T(8,128)(2,1)S(1)}, bf16[8,8192]{1,0:T(8,128)(2,1)S(1)}, u32[]{:S(2)}, u32[]{:S(2)}) collective-permute-start(bf16[8,8192]{1,0:T(8,128)(2,1)S(1)} %get-tuple-element.854), channel_id=1, source_target_pairs={{0,16},{16,32},{32,48},{48,64},{64,80},{80,96},{96,112},{112,128},... | collective-permute-start | bytes 393224 | tf_op jit(solution)/shard_map/while/body/eval_jaxpr/ppermute | solution.py:16
  946.9 19.3 %collective-permute-start = (bf16[8,8192]{1,0:T(8,128)(2,1)S(1)}, bf16[8,8192]{1,0:T(8,128)(2,1)S(1)}, u32[]{:S(2)}, u32[]{:S(2)}) collective-permute-start(bf16[8,8192]{1,0:T(8,128)(2,1)S(1)} %get-tuple-element.853), channel_id=1, source_target_pairs={{16,0},{32,16},{48,32},{64,48},{80,64},{96,80},{112,96},{128,112},... | collective-permute-start | bytes 393224 | tf_op jit(solution)/shard_map/while/body/eval_jaxpr/ppermute | solution.py:16
  980.2 19.3 %collective-permute-start = (bf16[8,8192]{1,0:T(8,128)(2,1)S(1)}, bf16[8,8192]{1,0:T(8,128)(2,1)S(1)}, u32[]{:S(2)}, u32[]{:S(2)}) collective-permute-start(bf16[8,8192]{1,0:T(8,128)(2,1)S(1)} %get-tuple-element.853), channel_id=1, source_target_pairs={{16,0},{32,16},{48,32},{64,48},{80,64},{96,80},{112,96},{128,112},... | collective-permute-start | bytes 393224 | tf_op jit(solution)/shard_map/while/body/eval_jaxpr/ppermute | solution.py:16
  982.2 18.8 %collective-permute-start.1 = (bf16[8,8192]{1,0:T(8,128)(2,1)S(1)}, bf16[8,8192]{1,0:T(8,128)(2,1)S(1)}, u32[]{:S(2)}, u32[]{:S(2)}) collective-permute-start(bf16[8,8192]{1,0:T(8,128)(2,1)S(1)} %get-tuple-element.854), channel_id=1, source_target_pairs={{0,16},{16,32},{32,48},{48,64},{64,80},{80,96},{96,112},{112,128},... | collective-permute-start | bytes 393224 | tf_op jit(solution)/shard_map/while/body/eval_jaxpr/ppermute | solution.py:16
  1014.1 20.6 %collective-permute-start = (bf16[8,8192]{1,0:T(8,128)(2,1)S(1)}, bf16[8,8192]{1,0:T(8,128)(2,1)S(1)}, u32[]{:S(2)}, u32[]{:S(2)}) collective-permute-start(bf16[8,8192]{1,0:T(8,128)(2,1)S(1)} %get-tuple-element.853), channel_id=1, source_target_pairs={{16,0},{32,16},{48,32},{64,48},{80,64},{96,80},{112,96},{128,112},... | collective-permute-start | bytes 393224 | tf_op jit(solution)/shard_map/while/body/eval_jaxpr/ppermute | solution.py:16
  1016.1 20.2 %collective-permute-start.1 = (bf16[8,8192]{1,0:T(8,128)(2,1)S(1)}, bf16[8,8192]{1,0:T(8,128)(2,1)S(1)}, u32[]{:S(2)}, u32[]{:S(2)}) collective-permute-start(bf16[8,8192]{1,0:T(8,128)(2,1)S(1)} %get-tuple-element.854), channel_id=1, source_target_pairs={{0,16},{16,32},{32,48},{48,64},{64,80},{80,96},{96,112},{112,128},... | collective-permute-start | bytes 393224 | tf_op jit(solution)/shard_map/while/body/eval_jaxpr/ppermute | solution.py:16
  1040.0 189.1 %reduce-scatter.9.cloned.1.call-start = ((), (), s32[]{:S(2)}) async-start(), calls=%async_computation.7 | async-start | bytes 2228224 | tf_op jit(solution)/shard_map/reduce_scatter | solution.py:202
  1043.9 253.9 %reduce-scatter.11.cloned.1.call-start = ((), (), s32[]{:S(2)}) async-start(), calls=%async_computation.8 | async-start | bytes 2228224 | tf_op jit(solution)/shard_map/reduce_scatter | solution.py:196
  1047.8 318.4 %reduce-scatter.5.cloned.1.call-start = ((), (), s32[]{:S(2)}) async-start(), calls=%async_computation.5 | async-start | bytes 2228224 | tf_op jit(solution)/shard_map/reduce_scatter | solution.py:193
  (162 other events, 743.0 us)
Sparse Core Ops, SparseCore 0:
  9.8 38.6 all-gather.8
  50.3 51.4 all-gather.6
  104.2 39.7 all-gather.10
  1040.1 121.1 reduce-scatter.6
  1163.7 65.3 reduce-scatter.8
  1231.5 66.2 reduce-scatter.10
  1300.3 65.8 reduce-scatter.4
